TPU v7x, 32 devices: a whole 2x2x4 slice. The times are simulated.
32 devices in a mesh: parts: 2 (over y), bank: 8 (over z, x), batch: 2 (over core).
Axes of the slice: x: 2, y: 2, z: 4, core: 2. Of those that a mesh axis runs over, the one named last changes fastest.
Arguments:
- bank: bfloat16 [32768, 256], P(('parts', 'bank')), parts along dimension 0, may hold values from -1 to 1
- queries: bfloat16 [4096, 256], P(('parts', 'batch')), parts along dimension 0, may hold values from -8 to 8
- keys: bfloat16 [4096, 256], P(('parts', 'batch')), parts along dimension 0, may hold values from -0.375 to 0.375
- labels: int32 [4096], P(('parts', 'batch')), parts along dimension 0, may hold values from 0 to 2047, each once
- mask_tiles: int32 [32, 16], P('parts'), parts along dimension 0, may hold values from 0 to 127
Outputs:
- new_bank: bfloat16 [32768, 256], P(('parts', 'bank')), parts along dimension 0
- query_grad: float32 [4096, 256], P(('parts', 'batch')), parts along dimension 0
- loss: float32 [4096], P(('parts', 'batch')), parts along dimension 0
There are 2 independent parts, one for each index of `parts`. A program takes and returns all parts, laid end to end along the dimension named above; each array names one. Nothing has to cross between parts.
Inputs may be any that keep to these rules, and one draw needn't show every extreme that they name: `labels`: a permutation: each row of keys is the positive of exactly one query. `mask_tiles`: tile t holds bank rows t * 128 to t * 128 + 127; row b lists tiles excluded for queries b * 128 to b * 128 + 127; numbers may repeat.
All inputs are finite; a program needn't handle non-finite values.
Results may differ from a plain program's by a relative error of at most 0.0055.
Values may be sent and summed in bfloat16 or wider, within the bound.
A program may use at most 64 MiB of HBM per device.

v0:
```python
import jax
import jax.numpy as jnp
from jax import lax
from jax.sharding import PartitionSpec as P

TILE = 128
TAU = 0.12
NEG = -1e30
EPS = 1e-06


def masked_scores(rows_q, rows_k, mask_rows, first):
    s = jnp.einsum("qd,kd->qk", rows_q, rows_k, preferred_element_type=jnp.float32) / TAU
    nq, nk = s.shape
    ids = first + jnp.arange(nk // TILE, dtype=jnp.int32)
    hit = jnp.any(mask_rows[:, :, None] == ids[None, None, :], axis=1)
    live = jnp.broadcast_to(
        jnp.logical_not(hit)[:, None, :, None], (nq // TILE, TILE, nk // TILE, TILE)
    ).reshape(nq, nk)
    return (jnp.where(live, s, NEG), live)


def on_device(bank, queries, keys, labels, mask_tiles):
    qdev = queries.shape[0]
    bdev = bank.shape[0]
    total_bank = bdev * lax.axis_size("bank")
    total_query = qdev * lax.axis_size("batch")
    eta = 0.25 * total_bank / total_query
    mine = lax.axis_index("batch")
    first = lax.axis_index("bank") * (bdev // TILE)
    all_keys = lax.all_gather(keys, "batch", axis=0, tiled=True)
    key_rows = jnp.take(all_keys, labels, axis=0)
    pos = jnp.sum(queries.astype(jnp.float32) * key_rows.astype(jnp.float32), axis=1) / TAU
    own_mask = lax.dynamic_slice_in_dim(mask_tiles, mine * (qdev // TILE), qdev // TILE, 0)
    scores, live = masked_scores(queries, bank, own_mask, first)
    top = lax.pmax(jnp.max(scores, axis=1), "bank")
    part_sum = jnp.sum(jnp.where(live, jnp.exp(scores - top[:, None]), 0.0), axis=1)
    total = lax.psum(part_sum, "bank")
    high = jnp.maximum(top, pos)
    lse = high + jnp.log(total * jnp.exp(top - high) + jnp.exp(pos - high))
    loss = lse - pos
    probs = jnp.exp(scores - lse[:, None]).astype(jnp.bfloat16)
    neg_local = jnp.dot(probs, bank, preferred_element_type=jnp.float32)
    own_pull = jnp.einsum("qk,qd->kd", probs, queries, preferred_element_type=jnp.float32)
    neg = lax.psum(neg_local, "bank")
    query_grad = (neg + (jnp.exp(pos - lse) - 1.0)[:, None] * key_rows.astype(jnp.float32)) / TAU
    pull = lax.psum(own_pull.astype(jnp.bfloat16), "batch").astype(jnp.float32)
    fresh = bank.astype(jnp.float32) + eta * pull
    fresh = fresh * lax.rsqrt(jnp.mean(fresh * fresh, axis=1, keepdims=True) + EPS)
    return (fresh.astype(jnp.bfloat16), query_grad, loss)


def solution(mesh):
    return jax.shard_map(
        on_device,
        mesh=mesh,
        in_specs=(
            P(("parts", "bank"), None),
            P(("parts", "batch"), None),
            P(("parts", "batch"), None),
            P(("parts", "batch")),
            P("parts", None),
        ),
        out_specs=(P(("parts", "bank"), None), P(("parts", "batch"), None), P(("parts", "batch"))),
        check_vma=False,
    )
```

profile of v0, /device:TPU:0, one launch (start us, length us, event | category | flops | bytes accessed | tf_op | source)
XLA Modules:
  0.0 187.6 jit_solution(10827751201215872760)
XLA Ops:
  7.2 0.0 copy-start
  7.2 0.0 all-gather.2.cloned.1.call-start
  7.2 0.7 all-gather.2.cloned.1.call-update
  7.9 0.0 all-reduce.3.cloned.1.call-start
  8.0 0.0 copy-done
  8.0 0.1 compare_reduce_fusion
  8.1 0.6 broadcast_in_dim.31
  8.7 6.8 %fusion = (f32[1024]{0:T(1024)S(1)}, f32[1024,2048]{1,0:T(8,128)}) fusion(pred[128,8,16,128]{3,2,1,0:T(8,128)(4,1)S(1)} %bitcast.17, bf16[1024,256]{1,0:T(8,128)(2,1)} %param.6, bf16[2048,256]{1,0:T(8,128)(2,1)} %param.5), kind=kOutput, calls=%fused_computation.4 | convolution fusion | flops 1080032256 | bytes 12062720 | tf_op jit(solution)/shard_map/qd,kd->qk/dot_general | solution.py:13
  15.5 23.1 %pmax.7 = f32[1024]{0:T(1024)S(1)} all-reduce(f32[1024]{0:T(1024)S(1)} %get-tuple-element.5), channel_id=1, replica_groups=mesh['parts'=2,'bank'=8,'batch'=2] {'bank'}, use_global_device_ids=true, to_apply=%region_2.3 | all-reduce | flops 1024 | bytes 8192 | tf_op jit(solution)/shard_map/pmax | solution.py:36
  38.6 5.3 %select_reduce_fusion = f32[1024]{0:T(1024)S(1)} fusion(pred[128,8,16,128]{3,2,1,0:T(8,128)(4,1)S(1)} %bitcast.18, f32[1024,2048]{1,0:T(8,128)} %get-tuple-element.6, f32[1024]{0:T(1024)S(1)} %pmax.7), kind=kLoop, calls=%fused_computation.2 | loop fusion | flops 10484736 | bytes 10493952 | tf_op jit(solution)/shard_map/reduce_sum | solution.py:37
  43.9 0.0 copy-start.3
  43.9 17.3 %psum.21 = f32[1024]{0:T(1024)S(1)} all-reduce(f32[1024]{0:T(1024)S(1)} %select_reduce_fusion), channel_id=1, replica_groups=mesh['parts'=2,'bank'=8,'batch'=2] {'bank'}, use_global_device_ids=true, to_apply=%region_5.6 | all-reduce | flops 1024 | bytes 8192 | tf_op jit(solution)/shard_map/psum | solution.py:38
  61.2 0.0 copy-done.4
  61.2 0.0 all-gather.2.cloned.1.call-done
  61.2 4.8 %gather_fusion = bf16[1024,256]{1,0:T(8,128)(2,1)S(1)} fusion(bf16[2048,256]{1,0:T(8,128)(2,1)} %all-gather.2.cloned.1.call-done, s32[1024]{0:T(1024)S(1)} %fusion.6), kind=kCustom, calls=%fused_computation | custom fusion | bytes 1052672 | tf_op jit(solution)/shard_map/jit(_take)/gather | solution.py:32
  66.1 0.0 copy-done.3
  66.1 0.5 fusion.1
  66.6 0.6 multiply_subtract_fusion
  67.2 5.5 %exponential_convert_fusion = bf16[1024,2048]{1,0:T(8,128)(2,1)S(1)} fusion(f32[1024,2048]{1,0:T(8,128)} %get-tuple-element.6, pred[128,8,16,128]{3,2,1,0:T(8,128)(4,1)S(1)} %bitcast.19, f32[1024]{0:T(1024)S(1)} %get-tuple-element.4), kind=kLoop, calls=%fused_computation.1 | loop fusion | flops 8388608 | bytes 14684160 | tf_op jit(solution)/shard_map/convert_element_type | solution.py:42
  72.7 0.0 copy-start.2
  72.7 1.9 %copy-done.2 = bf16[1024,2048]{1,0:T(8,128)(2,1)} copy-done((bf16[1024,2048]{1,0:T(8,128)(2,1)}, bf16[1024,2048]{1,0:T(8,128)(2,1)S(1)}, u32[]{:S(2)}) %copy-start.2) | copy-done | bytes 4194328
  74.6 2.4 %convolution_convert_fusion = bf16[2048,256]{1,0:T(8,128)(2,1)} fusion(bf16[1024,2048]{1,0:T(8,128)(2,1)S(1)} %exponential_convert_fusion, bf16[1024,256]{1,0:T(8,128)(2,1)S(1)} %copy-done.3), kind=kOutput, calls=%fused_computation.5 | convolution fusion | flops 1074266112 | bytes 5767168 | tf_op jit(solution)/shard_map/qk,qd->kd/dot_general | solution.py:44
  77.0 0.0 all-reduce.3.cloned.1.call-update
  77.0 0.0 all-reduce.5.cloned.1.call-start
  77.0 0.0 copy-done.1
  77.0 4.5 %fusion.7 = f32[1024,256]{1,0:T(8,128)} fusion(bf16[1024,2048]{1,0:T(8,128)(2,1)} %copy-done.2, bf16[2048,256]{1,0:T(8,128)(2,1)S(1)} %copy-done.1), kind=kOutput, calls=%fused_computation.28 | convolution fusion | flops 1073741824 | bytes 6291456 | tf_op jit(solution)/shard_map/dot_general | solution.py:43
  81.5 0.0 all-reduce.5.cloned.1.call-update
  81.6 13.9 %all-reduce.3.cloned.1.call-done = bf16[2048,256]{1,0:T(8,128)(2,1)} async-done(((bf16[2048,256]{1,0:T(8,128)(2,1)}), bf16[2048,256]{1,0:T(8,128)(2,1)}) %all-reduce.3.cloned.1.call-update) | async-done | bytes 1048592 | tf_op jit(solution)/shard_map/psum | solution.py:47
  95.5 1.7 multiply_reduce_fusion
  97.2 2.6 %multiply_convert_fusion = bf16[2048,256]{1,0:T(8,128)(2,1)} fusion(bf16[2048,256]{1,0:T(8,128)(2,1)} %all-reduce.3.cloned.1.call-done, bf16[2048,256]{1,0:T(8,128)(2,1)S(1)} %copy-done.1, f32[2048]{0:T(1024)S(1)} %add_rsqrt_fusion), kind=kLoop, calls=%fused_computation.6 | loop fusion | flops 3145728 | bytes 3153920 | tf_op jit(solution)/shard_map/convert_element_type | solution.py:50
  99.8 78.7 %all-reduce.5.cloned.1.call-done = f32[1024,256]{1,0:T(8,128)} async-done(((f32[1024,256]{1,0:T(8,128)}), f32[1024,256]{1,0:T(8,128)}) %all-reduce.5.cloned.1.call-update) | async-done | bytes 1048592 | tf_op jit(solution)/shard_map/psum | solution.py:45
  178.6 2.5 %fusion.3 = f32[1024,256]{1,0:T(8,128)} fusion(f32[1024,256]{1,0:T(8,128)} %all-reduce.5.cloned.1.call-done, f32[1024]{0:T(1024)S(1)} %exponential_add_fusion, bf16[1024,256]{1,0:T(8,128)(2,1)S(1)} %gather_fusion, pred[1024]{0:T(1024)(128)(4,1)S(1)} %compare_and_fusion), kind=kLoop, calls=%fused_computation.13 | loop fusion | flops 1310720 | bytes 2626560 | tf_op jit(solution)/shard_map/div | solution.py:46
  (9 shorter events, 0.1 us)
Async XLA Ops:
  7.2 0.8 copy-start
  7.2 54.1 %all-gather.2.cloned.1.call-start = ((), (), s32[]{:S(2)}) async-start(), calls=%async_computation | async-start | bytes 1572864 | tf_op jit(solution)/shard_map/all_gather | solution.py:31
  7.9 87.6 %all-reduce.3.cloned.1.call-start = ((), (), s32[]{:S(2)}) async-start(), calls=%async_computation.1 | async-start | bytes 2097152 | tf_op jit(solution)/shard_map/psum | solution.py:47
  38.6 22.6 %copy-start.4 = (s32[1024]{0:T(1024)S(1)}, s32[1024]{0:T(1024)}, u32[]{:S(2)}) copy-start(s32[1024]{0:T(1024)} %param.8) | copy-start | bytes 12292
  43.9 22.2 %copy-start.3 = (bf16[1024,256]{1,0:T(8,128)(2,1)S(1)}, bf16[1024,256]{1,0:T(8,128)(2,1)}, u32[]{:S(2)}) copy-start(bf16[1024,256]{1,0:T(8,128)(2,1)} %param.6) | copy-start | bytes 1572868
  72.7 1.9 %copy-start.2 = (bf16[1024,2048]{1,0:T(8,128)(2,1)}, bf16[1024,2048]{1,0:T(8,128)(2,1)S(1)}, u32[]{:S(2)}) copy-start(bf16[1024,2048]{1,0:T(8,128)(2,1)S(1)} %exponential_convert_fusion) | copy-start | bytes 12582916
  74.6 2.4 %copy-start.1 = (bf16[2048,256]{1,0:T(8,128)(2,1)S(1)}, bf16[2048,256]{1,0:T(8,128)(2,1)}, u32[]{:S(2)}) copy-start(bf16[2048,256]{1,0:T(8,128)(2,1)} %param.5) | copy-start | bytes 3145732
  77.0 101.6 %all-reduce.5.cloned.1.call-start = ((), (), s32[]{:S(2)}) async-start(), calls=%async_computation.2 | async-start | bytes 2097152 | tf_op jit(solution)/shard_map/psum | solution.py:45
Sparse Core Ops, SparseCore 0:
  9.6 11.7 all-gather.1
  77.1 18.3 all-reduce.2
  99.4 79.1 all-reduce.4
where the time goes:
time: 188 us
  waiting for transfers between devices  93.4 us (50%)
  blocking collectives  40.3 us (21%)
  other arithmetic  18.9 us (10%)
  between operations  13.9 us (7%)
  matrix products  13.6 us (7%)
  local copies, waits for them, and re-layouts  7.38 us (4%)
    psum x1, waiting for transfers between devices, on_device(): neg = lax.psum(neg_local, 'bank')  78.7 us
    pmax x1, blocking collectives, on_device(): top = lax.pmax(jnp.max(scores, axis=1), 'bank')  23.1 us
    psum x1, blocking collectives, on_device(): total = lax.psum(part_sum, 'bank')  17.3 us
    psum x1, waiting for transfers between devices, on_device(): pull = lax.psum(own_pull.astype(jnp.bfloat16), 'batch').astype(jnp.float32)  13.9 us
    dot_general x1, matrix products, masked_scores(): jnp.einsum('qd,kd->qk', rows_q, rows_k, preferred_element_type=jnp.float32)  6.76 us
    convert_element_type x1, other arithmetic, on_device(): probs = jnp.exp(scores - lse[:, None]).astype(jnp.bfloat16)  5.45 us
    reduce_sum x1, other arithmetic, on_device(): jnp.sum(jnp.where(live, jnp.exp(scores - top[:, None]), 0.0), axis=1)  5.32 us
    gather x1, local copies, waits for them, and re-layouts, on_device(): key_rows = jnp.take(all_keys, labels, axis=0)  4.82 us
  transfers between devices with their start and end apart: 3, of which 2 were waited for; matrix products, arithmetic and copies ran while one was open for 12% of the time, Pallas kernels for 0%

commit v1 on v0

--- a/solution.py
+++ b/solution.py
@@ -7,6 +7,11 @@
 TAU = 0.12
 NEG = -1e30
 EPS = 1e-06
+
+
+def add_all(x, axis):
+    terms = lax.all_gather(x, axis)
+    return jnp.sum(terms, axis=0)
 
 
 def masked_scores(rows_q, rows_k, mask_rows, first):
@@ -44,7 +49,7 @@
     own_pull = jnp.einsum("qk,qd->kd", probs, queries, preferred_element_type=jnp.float32)
     neg = lax.psum(neg_local, "bank")
     query_grad = (neg + (jnp.exp(pos - lse) - 1.0)[:, None] * key_rows.astype(jnp.float32)) / TAU
-    pull = lax.psum(own_pull.astype(jnp.bfloat16), "batch").astype(jnp.float32)
+    pull = add_all(own_pull.astype(jnp.bfloat16), "batch").astype(jnp.float32)
     fresh = bank.astype(jnp.float32) + eta * pull
     fresh = fresh * lax.rsqrt(jnp.mean(fresh * fresh, axis=1, keepdims=True) + EPS)
     return (fresh.astype(jnp.bfloat16), query_grad, loss)

time: 188 us -> 178 us (0.947)
  waiting for transfers between devices: 93.4 us -> 82.7 us
    psum x1 -> x0, waiting for transfers between devices: 13.9 us -> none  [on_device(): pull = lax.psum(own_pull.astype(jnp.bfloat16), 'batch').astype(jnp.float32)]
    all_gather x0 -> x1, waiting for transfers between devices: none -> 9.87 us  [add_all(): terms = lax.all_gather(x, axis)]
    psum x1, waiting for transfers between devices: 78.7 us -> 72.1 us  [on_device(): neg = lax.psum(neg_local, 'bank')]
    reduce_sum x0 -> x1, other arithmetic: none -> 2.64 us  [add_all(): return jnp.sum(terms, axis=0)]
    dot_general x1, matrix products: 4.47 us -> 2.22 us  [on_device(): neg_local = jnp.dot(probs, bank, preferred_element_type=jnp.float32)]
    dot_general x1, matrix products: 2.37 us -> 4.51 us  [on_device(): jnp.einsum('qk,qd->kd', probs, queries, preferred_element_type=jnp.float32)]
  transfers between devices with their start and end apart: 3 -> 3, of which waited for: 2 -> 2; matrix products, arithmetic and copies ran while one was open for 12% -> 11% of each run, Pallas kernels for 0% -> 0%
where the time goes in v1:
time: 178 us; the launch traced here: 177 us
  waiting for transfers between devices  82.7 us (46%)
  blocking collectives  40.3 us (23%)
  other arithmetic  19.2 us (11%)
  between operations  13.9 us (8%)
  matrix products  13.5 us (8%)
  local copies, waits for them, and re-layouts  7.39 us (4%)
    psum x1, waiting for transfers between devices, on_device(): neg = lax.psum(neg_local, 'bank')  72.1 us
    pmax x1, blocking collectives, on_device(): top = lax.pmax(jnp.max(scores, axis=1), 'bank')  23.1 us
    psum x1, blocking collectives, on_device(): total = lax.psum(part_sum, 'bank')  17.3 us
    all_gather x1, waiting for transfers between devices, add_all(): terms = lax.all_gather(x, axis)  9.87 us
    dot_general x1, matrix products, masked_scores(): jnp.einsum('qd,kd->qk', rows_q, rows_k, preferred_element_type=jnp.float32)  6.76 us
    convert_element_type x1, other arithmetic, on_device(): probs = jnp.exp(scores - lse[:, None]).astype(jnp.bfloat16)  5.54 us
    reduce_sum x1, other arithmetic, on_device(): jnp.sum(jnp.where(live, jnp.exp(scores - top[:, None]), 0.0), axis=1)  5.32 us
    gather x1, local copies, waits for them, and re-layouts, on_device(): key_rows = jnp.take(all_keys, labels, axis=0)  4.82 us
  transfers between devices with their start and end apart: 3, of which 2 were waited for; matrix products, arithmetic and copies ran while one was open for 11% of the time, Pallas kernels for 0%

profile of v1, /device:TPU:0, one launch (start us, length us, event | category | flops | bytes accessed | tf_op | source)
XLA Modules:
  0.0 177.3 jit_solution(5425298959721711608)
XLA Ops:
  7.2 0.0 copy-start
  7.2 0.0 all-gather.4.cloned.1.call-start
  7.2 0.7 all-gather.4.cloned.1.call-update
  7.9 0.0 all-reduce.2.cloned.1.call-start
  8.0 0.1 compare_reduce_fusion
  8.1 0.6 broadcast_in_dim.31
  8.7 6.8 %fusion = (f32[1024]{0:T(1024)S(1)}, f32[1024,2048]{1,0:T(8,128)}) fusion(pred[128,8,16,128]{3,2,1,0:T(8,128)(4,1)S(1)} %bitcast.18, bf16[1024,256]{1,0:T(8,128)(2,1)} %param.6, bf16[2048,256]{1,0:T(8,128)(2,1)} %param.5), kind=kOutput, calls=%fused_computation.4 | convolution fusion | flops 1080032256 | bytes 12062720 | tf_op jit(solution)/shard_map/qd,kd->qk/dot_general | solution.py:18
  15.5 23.1 %pmax.7 = f32[1024]{0:T(1024)S(1)} all-reduce(f32[1024]{0:T(1024)S(1)} %get-tuple-element.5), channel_id=1, replica_groups=mesh['parts'=2,'bank'=8,'batch'=2] {'bank'}, use_global_device_ids=true, to_apply=%region_2.3 | all-reduce | flops 1024 | bytes 8192 | tf_op jit(solution)/shard_map/pmax | solution.py:41
  38.6 5.3 %select_reduce_fusion = f32[1024]{0:T(1024)S(1)} fusion(pred[128,8,16,128]{3,2,1,0:T(8,128)(4,1)S(1)} %bitcast.19, f32[1024,2048]{1,0:T(8,128)} %get-tuple-element.6, f32[1024]{0:T(1024)S(1)} %pmax.7), kind=kLoop, calls=%fused_computation.2 | loop fusion | flops 10484736 | bytes 10493952 | tf_op jit(solution)/shard_map/reduce_sum | solution.py:42
  43.9 0.0 copy-start.4
  43.9 17.3 %psum.14 = f32[1024]{0:T(1024)S(1)} all-reduce(f32[1024]{0:T(1024)S(1)} %select_reduce_fusion), channel_id=1, replica_groups=mesh['parts'=2,'bank'=8,'batch'=2] {'bank'}, use_global_device_ids=true, to_apply=%region_5.6 | all-reduce | flops 1024 | bytes 8192 | tf_op jit(solution)/shard_map/psum | solution.py:43
  61.2 0.0 all-gather.4.cloned.1.call-done
  61.2 4.8 %gather_fusion = bf16[1024,256]{1,0:T(8,128)(2,1)S(1)} fusion(bf16[2048,256]{1,0:T(8,128)(2,1)} %all-gather.4.cloned.1.call-done, s32[1024]{0:T(1024)S(1)} %fusion.6), kind=kCustom, calls=%fused_computation | custom fusion | bytes 1052672 | tf_op jit(solution)/shard_map/jit(_take)/gather | solution.py:37
  66.1 0.0 copy-done.4
  66.1 0.5 fusion.1
  66.6 0.6 multiply_subtract_fusion
  67.2 5.5 %exponential_convert_fusion = bf16[1024,2048]{1,0:T(8,128)(2,1)S(1)} fusion(f32[1024,2048]{1,0:T(8,128)} %get-tuple-element.6, pred[128,8,16,128]{3,2,1,0:T(8,128)(4,1)S(1)} %bitcast.20, f32[1024]{0:T(1024)S(1)} %get-tuple-element.4), kind=kLoop, calls=%fused_computation.1 | loop fusion | flops 8388608 | bytes 14684160 | tf_op jit(solution)/shard_map/convert_element_type | solution.py:47
  72.8 0.0 copy-start.3
  72.8 1.9 %copy-done.3 = bf16[1024,2048]{1,0:T(8,128)(2,1)} copy-done((bf16[1024,2048]{1,0:T(8,128)(2,1)}, bf16[1024,2048]{1,0:T(8,128)(2,1)S(1)}, u32[]{:S(2)}) %copy-start.3) | copy-done | bytes 4194328
  74.7 0.0 copy-done.1
  74.7 2.2 %fusion.7 = f32[1024,256]{1,0:T(8,128)} fusion(bf16[1024,2048]{1,0:T(8,128)(2,1)S(1)} %exponential_convert_fusion, bf16[2048,256]{1,0:T(8,128)(2,1)S(1)} %copy-done.1), kind=kOutput, calls=%fused_computation.28 | convolution fusion | flops 1073741824 | bytes 6291456 | tf_op jit(solution)/shard_map/dot_general | solution.py:48
  76.9 0.0 all-reduce.2.cloned.1.call-update
  76.9 0.2 all-gather.6.cloned.1.call-start
  77.2 4.5 %convolution_convert_fusion = bf16[2048,256]{1,0:T(8,128)(2,1)} fusion(bf16[1024,2048]{1,0:T(8,128)(2,1)} %copy-done.3, bf16[1024,256]{1,0:T(8,128)(2,1)S(1)} %copy-done.4), kind=kOutput, calls=%fused_computation.5 | convolution fusion | flops 1074266112 | bytes 5767168 | tf_op jit(solution)/shard_map/qk,qd->kd/dot_general | solution.py:49
  81.7 0.0 all-gather.6.cloned.1.call-update
  81.7 72.1 %all-reduce.2.cloned.1.call-done = f32[1024,256]{1,0:T(8,128)} async-done(((f32[1024,256]{1,0:T(8,128)}), f32[1024,256]{1,0:T(8,128)}) %all-reduce.2.cloned.1.call-update) | async-done | bytes 1048592 | tf_op jit(solution)/shard_map/psum | solution.py:50
  153.8 2.5 %fusion.3 = f32[1024,256]{1,0:T(8,128)} fusion(f32[1024,256]{1,0:T(8,128)} %all-reduce.2.cloned.1.call-done, f32[1024]{0:T(1024)S(1)} %exponential_add_fusion, bf16[1024,256]{1,0:T(8,128)(2,1)S(1)} %gather_fusion, pred[1024]{0:T(1024)(128)(4,1)S(1)} %compare_and_fusion), kind=kLoop, calls=%fused_computation.13 | loop fusion | flops 1310720 | bytes 2626560 | tf_op jit(solution)/shard_map/div | solution.py:51
  156.4 9.9 %all-gather.6.cloned.1.call-done = bf16[4096,256]{1,0:T(8,128)(2,1)} async-done(((bf16[2048,256]{1,0:T(8,128)(2,1)}), bf16[4096,256]{1,0:T(8,128)(2,1)}) %all-gather.6.cloned.1.call-update) | async-done | bytes 2097168 | tf_op jit(solution)/shard_map/all_gather | solution.py:13
  166.2 2.6 %reduce_sum.41 = bf16[2048,256]{1,0:T(8,128)(2,1)S(1)} reduce(bf16[2,2048,256]{2,1,0:T(8,128)(2,1)} %bitcast.21, bf16[]{:T(256)} %constant.51.clone.1), dimensions={0}, to_apply=%region_6.7 | reduce | flops 524288 | bytes 3145730 | tf_op jit(solution)/shard_map/reduce_sum | solution.py:14
  168.9 0.0 copy-done.2
  168.9 0.5 multiply_reduce_fusion
  169.4 1.4 multiply_convert_fusion
  (12 shorter events, 0.1 us)
Async XLA Ops:
  7.2 0.8 copy-start
  7.2 54.1 %all-gather.4.cloned.1.call-start = ((), (), s32[]{:S(2)}) async-start(), calls=%async_computation | async-start | bytes 1572864 | tf_op jit(solution)/shard_map/all_gather | solution.py:36
  7.9 145.9 %all-reduce.2.cloned.1.call-start = ((), (), s32[]{:S(2)}) async-start(), calls=%async_computation.1 | async-start | bytes 2097152 | tf_op jit(solution)/shard_map/psum | solution.py:50
  38.6 22.6 %copy-start.5 = (s32[1024]{0:T(1024)S(1)}, s32[1024]{0:T(1024)}, u32[]{:S(2)}) copy-start(s32[1024]{0:T(1024)} %param.8) | copy-start | bytes 12292
  43.9 22.2 %copy-start.4 = (bf16[1024,256]{1,0:T(8,128)(2,1)S(1)}, bf16[1024,256]{1,0:T(8,128)(2,1)}, u32[]{:S(2)}) copy-start(bf16[1024,256]{1,0:T(8,128)(2,1)} %param.6) | copy-start | bytes 1572868
  67.2 7.5 %copy-start.1 = (bf16[2048,256]{1,0:T(8,128)(2,1)S(1)}, bf16[2048,256]{1,0:T(8,128)(2,1)}, u32[]{:S(2)}) copy-start(bf16[2048,256]{1,0:T(8,128)(2,1)} %param.5) | copy-start | bytes 3145732
  72.8 1.9 %copy-start.3 = (bf16[1024,2048]{1,0:T(8,128)(2,1)}, bf16[1024,2048]{1,0:T(8,128)(2,1)S(1)}, u32[]{:S(2)}) copy-start(bf16[1024,2048]{1,0:T(8,128)(2,1)S(1)} %exponential_convert_fusion) | copy-start | bytes 12582916
  76.9 89.3 %all-gather.6.cloned.1.call-start = ((), (), s32[]{:S(2)}) async-start(), calls=%async_computation.2 | async-start | bytes 3145728 | tf_op jit(solution)/shard_map/all_gather | solution.py:13
  81.7 87.2 %copy-start.2 = (bf16[2048,256]{1,0:T(8,128)(2,1)S(1)}, bf16[2048,256]{1,0:T(8,128)(2,1)}, u32[]{:S(2)}) copy-start(bf16[2048,256]{1,0:T(8,128)(2,1)} %param.5) | copy-start | bytes 3145732
Sparse Core Ops, SparseCore 0:
  9.6 11.7 all-gather.3
  77.1 76.7 all-reduce.1
  156.0 10.1 all-gather.5
